TPU v7x, 128 devices: a whole 4x4x4 slice. The times are simulated.
128 devices in a mesh: grp: 4 (over z), dev: 32 (over y, x, core).
Axes of the slice: x: 4, y: 4, z: 4, core: 2. Of those that a mesh axis runs over, the one named last changes fastest.
Arguments:
- hidden_rows: bfloat16 [1024, 7168], P(('grp', 'dev')), may hold values from -6 to 6
- queries: bfloat16 [1024, 128, 576], P(('grp', 'dev')), may hold values from -320 to 320
- kv_cache: bfloat16 [1024, 512, 576], P(('grp', 'dev')), may hold values from -4 to 4
- cache_lengths: int32 [1024], P(('grp', 'dev')), may hold values from 2 to 512, as said below
- value_lift: bfloat16 [128, 512, 128], P('dev'), may hold values from -0.25 to 0.25
- out_weight: bfloat16 [128, 128, 7168], P('dev'), may hold values from -0.046875 to 0.046875
- expert_ids: int32 [1024, 8], P(('grp', 'dev')), may hold values from 0 to 31, all different within a row; in each aligned block of 4 rows (0 to 3, 4 to 7, ...) at most 2 rows name the same one
- weight_codes: int32 [1024, 8], P(('grp', 'dev')), may hold values from 1 to 255
- w_gate: bfloat16 [32, 7168, 1024], P('dev', None, 'grp'), may hold values from -0.0625 to 0.0625
- w_up: bfloat16 [32, 7168, 1024], P('dev', None, 'grp'), may hold values from -0.0625 to 0.0625
- w_down: bfloat16 [32, 1024, 7168], P('dev', 'grp'), may hold values from -0.1875 to 0.1875
Outputs:
- layer_out: bfloat16 [1024, 7168], P(('grp', 'dev'))
Inputs may be any that keep to these rules, and one draw needn't show every extreme that they name: `expert_ids`: each row names 8 different experts; in each aligned block of 4 rows no expert is named by more than 2 rows, and in some block one expert is named by exactly 2. `cache_lengths`: some request has exactly 512 live positions.
All inputs are finite; a program needn't handle non-finite values.
Results may differ from a plain program's by a relative error of at most 0.012.
Values may be sent and summed in bfloat16 or wider, within the bound.
No kernel may reach another device: no remote copies, remote signals or barrier semaphores. Data moves between devices by JAX's collectives and lax.ppermute only.
A program may use at most 128 MiB of HBM per device.

v0:
```python
import jax
import jax.numpy as jnp
from jax import lax
from jax.experimental import pallas as pl
from jax.experimental.pallas import tpu as pltpu
from jax.sharding import PartitionSpec as P


LATENT = 512
SCALE = 192.0 ** (-0.5)
ALL = ("grp", "dev")
BF = jnp.bfloat16
F32 = jnp.float32


def place(i):
    return [i // 32, (i // 8) % 4, (i // 2) % 4, i % 2]


def number(at):
    return ((at[0] * 4 + at[1]) * 4 + at[2]) * 2 + at[3]


def core_pairs():
    return [(i, i ^ 1) for i in range(128)]


def ring_pairs(axis, step):
    pairs = []
    for i in range(128):
        at = place(i)
        flip = (1, 3) if at[3] == 0 else (3, 1)
        at[axis] ^= flip[step]
        pairs.append((i, number(at)))
    return pairs


Z, Y, X = 0, 1, 2


def swap(value, axis, step):
    return lax.ppermute(value, ALL, ring_pairs(axis, step))


def other_core(value):
    return lax.ppermute(value, ALL, core_pairs())


PER_STEP = 2


def attend_kernel(length_ref, q_ref, kv_ref, out_ref):
    for j in range(PER_STEP):
        kv = kv_ref[j]
        logits = lax.dot_general(
            q_ref[j], kv, (((0,), (0,)), ((), ())), preferred_element_type=F32
        ) * SCALE
        live = lax.broadcasted_iota(jnp.int32, logits.shape, 1) < length_ref[
            pl.program_id(0) * PER_STEP + j
        ]
        logits = jnp.where(live, logits, -jnp.inf)
        exponent = jnp.exp(logits - jnp.max(logits, axis=1, keepdims=True))
        soft = (exponent / jnp.sum(exponent, axis=1, keepdims=True)).astype(BF)
        result = lax.dot_general(
            soft, kv[:LATENT], (((1,), (1,)), ((), ())), preferred_element_type=F32
        )
        out_ref[:, j] = result.astype(BF).reshape(out_ref.shape[0], out_ref.shape[2], LATENT)


def attend(queries, kv_cache, cache_lengths):
    rows, heads, depth = queries.shape
    live = kv_cache.shape[1]
    return pl.pallas_call(
        attend_kernel,
        grid_spec=pltpu.PrefetchScalarGridSpec(
            num_scalar_prefetch=1,
            grid=(rows // PER_STEP,),
            in_specs=[
                pl.BlockSpec((PER_STEP, depth, heads), lambda i, n: (i, 0, 0)),
                pl.BlockSpec((PER_STEP, depth, live), lambda i, n: (i, 0, 0)),
            ],
            out_specs=pl.BlockSpec((16, PER_STEP, heads // 16, LATENT), lambda i, n: (0, i, 0, 0)),
        ),
        out_shape=jax.ShapeDtypeStruct((16, rows, heads // 16, LATENT), BF),
        name="attend",
    )(cache_lengths, jnp.swapaxes(queries, 1, 2), jnp.swapaxes(kv_cache, 1, 2))


def project_kernel(steps, left_in, right_in, own_ref, other_ref, left_ref, right_ref):
    depth = own_ref.shape[0]

    def run(rows_ref, out_ref):
        out_ref[...] = (
            jnp.dot(rows_ref[:, :depth], own_ref[...], preferred_element_type=F32)
            + jnp.dot(rows_ref[:, depth:], other_ref[...], preferred_element_type=F32)
        ).astype(BF)

    @pl.when(pl.program_id(0) < steps)
    def _():
        run(left_in, left_ref)

    @pl.when(pl.program_id(0) >= steps)
    def _():
        run(right_in, right_ref)


def project(left_in, right_in, own, other):
    rows, depth = left_in.shape
    width = own.shape[1]
    block = 896
    steps = width // 2 // block
    whole = pl.BlockSpec((rows, depth), lambda i: (0, 0))
    matrix = pl.BlockSpec((depth // 2, block), lambda i: (0, i))
    shape = jax.ShapeDtypeStruct((rows, width // 2), BF)
    return pl.pallas_call(
        lambda *refs: project_kernel(steps, *refs),
        grid=(2 * steps,),
        in_specs=[whole, whole, matrix, matrix],
        out_specs=[
            pl.BlockSpec((rows, block), lambda i: (0, jnp.minimum(i, steps - 1))),
            pl.BlockSpec((rows, block), lambda i: (0, jnp.maximum(i - steps, 0))),
        ],
        out_shape=[shape, shape],
        name="project",
    )(left_in, right_in, own, other)


BLOCK = 1024


def experts_kernel(
    steps, number_ref, xa, xb, ra, rb, gate_own, gate_other, up_own, up_other,
    down_own, down_other, out_a, out_b, acc, hidden,
):
    step = pl.program_id(0)
    units = gate_own.shape[1]

    @pl.when(step == 0)
    def _():
        acc[...] = jnp.zeros_like(acc)

    @pl.when(step < steps)
    def _():
        rows = jnp.concatenate([xa[...], xb[...]], axis=0)
        for at, matrix in enumerate((gate_own, up_own, gate_other, up_other)):
            acc[:, at * units : (at + 1) * units] += jnp.dot(
                rows, matrix[...], preferred_element_type=F32
            )

    @pl.when(step == steps - 1)
    def _():
        table = jnp.concatenate([ra[...], rb[...]], axis=0).astype(F32)
        ids, codes = table[:, :8], table[:, 8:16]
        weights = 2.5 * codes / jnp.sum(codes, axis=1, keepdims=True)
        for at in range(2):
            named = ids == (number_ref[at]).astype(F32)
            share = jnp.sum(jnp.where(named, weights, 0.0), axis=1, keepdims=True)
            gate = acc[:, 2 * at * units : (2 * at + 1) * units]
            up = acc[:, (2 * at + 1) * units : (2 * at + 2) * units]
            value = gate / (1.0 + jnp.exp(-gate)) * up * share
            hidden[:, at * units : (at + 1) * units] = value.astype(BF)

    @pl.when(step >= steps)
    def _():
        result = jnp.dot(
            hidden[:, :units], down_own[...], preferred_element_type=F32
        ) + jnp.dot(hidden[:, units:], down_other[...], preferred_element_type=F32)
        half = result.shape[0] // 2
        out_a[...] = result[:half].astype(BF)
        out_b[...] = result[half:].astype(BF)


def experts(numbers, xa, xb, weights, width):
    rows = xa.shape[0]
    units = weights[0].shape[2]
    steps = width // BLOCK
    first = lambda i, n: (0, jnp.minimum(i, steps - 1))
    routing = pl.BlockSpec((rows, 128), lambda i, n: (0, width // 128))
    into = pl.BlockSpec(
        (pl.Squeezed(), BLOCK, units), lambda i, n: (0, jnp.minimum(i, steps - 1), 0)
    )
    onward = pl.BlockSpec(
        (pl.Squeezed(), units, BLOCK), lambda i, n: (0, 0, jnp.maximum(i - steps, 0))
    )
    back = pl.BlockSpec((rows, BLOCK), lambda i, n: (0, jnp.maximum(i - steps, 0)))
    shape = jax.ShapeDtypeStruct((rows, width), BF)
    return pl.pallas_call(
        lambda *refs: experts_kernel(steps, *refs),
        grid_spec=pltpu.PrefetchScalarGridSpec(
            num_scalar_prefetch=1,
            grid=(2 * steps,),
            in_specs=[
                pl.BlockSpec((rows, BLOCK), first),
                pl.BlockSpec((rows, BLOCK), first),
                routing,
                routing,
                into,
                into,
                into,
                into,
                onward,
                onward,
            ],
            out_specs=[back, back],
            scratch_shapes=[
                pltpu.VMEM((2 * rows, 4 * units), F32),
                pltpu.VMEM((2 * rows, 2 * units), BF),
            ],
        ),
        out_shape=[shape, shape],
        name="experts",
    )(numbers, xa, xb, xa, xb, *weights)


def ring_offset(bits, core):
    low, high = bits % 2, bits // 2
    first = jnp.where(core == 0, 1, 3)
    second = jnp.where(core == 0, 3, 1)
    return (low * first) ^ (high * second)


def plane_order(rows, here, core, y_first):
    count = rows // 16
    at = jnp.arange(rows, dtype=jnp.int32)
    block = at // count
    major, minor = block // 4, block % 4
    y = (here // 4) ^ ring_offset(major if y_first else minor, core)
    x = (here % 4) ^ ring_offset(minor if y_first else major, core)
    source = (y * 4 + x) * count + at % count
    return (source[:, None] == jnp.arange(rows, dtype=jnp.int32)[None, :]).astype(BF)


def halves(value):
    half = value.shape[0] // 2
    return value[:half], value[half:]


def fold(value, axis, step):
    keep, send = halves(value)
    got = swap(send, axis, step)
    return (keep.astype(F32) + got.astype(F32)).astype(BF)


def grow(value, axis, step):
    return jnp.concatenate([value, swap(value, axis, step)], axis=0)


def run_rows(
    hidden_rows,
    queries,
    kv_cache,
    cache_lengths,
    value_lift,
    out_weight,
    expert_ids,
    weight_codes,
    w_gate,
    w_up,
    w_down,
):
    device = lax.axis_index("dev")
    core = device % 2
    here = device // 2
    _, width = hidden_rows.shape

    swapped = []
    for matrix in (value_lift, out_weight, w_gate, w_up, w_down):
        swapped.append(other_core(matrix))
    lift_other, out_other, gate_other, up_other, down_other = swapped

    heads_out = attend(queries, kv_cache, cache_lengths)
    same_core = [[c + 2 * i for i in range(16)] for c in range(2)]
    moved = lax.all_to_all(
        heads_out, "dev", split_axis=0, concat_axis=0, tiled=True, axis_index_groups=same_core
    )
    all_rows = moved.shape[0] * moved.shape[1]
    moved = moved.reshape(all_rows, moved.shape[2], LATENT)
    own = lax.dynamic_slice_in_dim(moved, 4 * core, 4, 1)
    other = lax.dynamic_slice_in_dim(moved, 4 * (1 - core), 4, 1)

    def lifted(part, lift):
        return jnp.einsum("rhl,hlv->rhv", part, lift, preferred_element_type=F32).astype(BF)

    head_values = jnp.concatenate(
        [lifted(own, value_lift), lifted(other, lift_other)], axis=1
    ).reshape(all_rows, -1)

    def ordered(y_first):
        order = plane_order(all_rows, here, core, y_first)
        return jnp.dot(order, head_values, preferred_element_type=F32).astype(BF)

    left, right = project(
        ordered(True),
        ordered(False),
        out_weight.reshape(-1, width),
        out_other.reshape(-1, width),
    )
    for axis_left, axis_right, step in ((Y, X, 1), (Y, X, 0), (X, Y, 1), (X, Y, 0)):
        left = fold(left, axis_left, step)
        right = fold(right, axis_right, step)
    attention = jnp.concatenate([left, right], axis=1).astype(F32)
    residual = hidden_rows.astype(F32) + attention
    normed = (
        residual * lax.rsqrt(jnp.mean(residual * residual, axis=1, keepdims=True) + 1e-06)
    ).astype(BF)

    routing = jnp.concatenate([expert_ids, weight_codes], axis=1).astype(BF)
    routing = jnp.pad(routing, ((0, 0), (0, 128 - routing.shape[1])))
    first = grow(jnp.concatenate([normed, routing], axis=1), Z, 0)
    second = swap(first, Z, 1)
    for axis_first, axis_second, step in ((X, Y, 0), (X, Y, 1), (Y, X, 0)):
        first = grow(first, axis_first, step)
        second = grow(second, axis_second, step)
    first_far = swap(first, Y, 1)
    second_far = swap(second, X, 1)

    numbers = jnp.stack([device, device ^ 1]).astype(jnp.int32)
    weights = (w_gate, gate_other, w_up, up_other, w_down, down_other)
    out_first, out_second = experts(numbers, first, second, weights, width)
    out_first_far, out_second_far = experts(numbers, first_far, second_far, weights, width)

    def add(one, two):
        return (one.astype(F32) + two.astype(F32)).astype(BF)

    out_first = add(out_first, swap(out_first_far, Y, 1))
    out_second = add(out_second, swap(out_second_far, X, 1))
    for axis_first, axis_second, step in ((Y, X, 0), (X, Y, 1), (X, Y, 0)):
        out_first = fold(out_first, axis_first, step)
        out_second = fold(out_second, axis_second, step)
    combined = add(out_first, swap(out_second, Z, 1))
    keep, send = halves(combined)
    combined = keep.astype(F32) + swap(send, Z, 0).astype(F32)
    return (residual + combined).astype(BF)


def solution(mesh):
    both = P(ALL, None)
    in_specs = (
        both,
        P(ALL, None, None),
        P(ALL, None, None),
        P(ALL),
        P("dev", None, None),
        P("dev", None, None),
        both,
        both,
        P("dev", None, "grp"),
        P("dev", None, "grp"),
        P("dev", "grp", None),
    )
    return jax.shard_map(run_rows, mesh=mesh, in_specs=in_specs, out_specs=both, check_vma=False)
```

profile of v0, /device:TPU:0, one launch (start us, length us, event | category | flops | bytes accessed | tf_op | source)
XLA Modules:
  0.0 266.8 jit_solution(10472870553744495348)
XLA Ops:
  0.0 8.0 %attend.1 = bf16[16,8,8,512]{3,2,1,0:T(8,128)(2,1)} custom-call(s32[8]{0:T(128)} %length_ref.1, bf16[8,576,128]{2,1,0:T(8,128)(2,1)} %bitcast.21, bf16[8,576,512]{2,1,0:T(8,128)(2,1)} %bitcast.17), custom_call_target="tpu_custom_call" | custom-call | tf_op jit(solution)/shard_map/attend/pallas_call | solution.py:73
  8.0 7.3 %all-to-all-start = ((bf16[16,8,8,512]{3,2,1,0:T(8,128)(2,1)}), bf16[16,8,8,512]{3,2,1,0:T(8,128)(2,1)S(1)}, u32[]{:S(2)}, u32[]{:S(2)}) async-start(bf16[16,8,8,512]{3,2,1,0:T(8,128)(2,1)} %attend.1), calls=%async_computation | async-start | bytes 2097152 | tf_op jit(solution)/shard_map/all_to_all | solution.py:273
  15.8 18.1 %all-to-all-done = bf16[16,8,8,512]{3,2,1,0:T(8,128)(2,1)S(1)} async-done(((bf16[16,8,8,512]{3,2,1,0:T(8,128)(2,1)}), bf16[16,8,8,512]{3,2,1,0:T(8,128)(2,1)S(1)}, u32[]{:S(2)}, u32[]{:S(2)}) %all-to-all-start) | async-done | bytes 1048608 | tf_op jit(solution)/shard_map/all_to_all | solution.py:273
  37.1 10.0 %project.1 = (bf16[128,3584]{1,0:T(8,128)(2,1)}, bf16[128,3584]{1,0:T(8,128)(2,1)}) custom-call(bf16[128,1024]{1,0:T(8,128)(2,1)} %convolution_convert_fusion.1.refs_0_, bf16[128,1024]{1,0:T(8,128)(2,1)} %convolution_convert_fusion.refs_1_, bf16[512,7168]{1,0:T(8,128)(2,1)} %bitcast.16, bf16[512,7168]{1,0:T(8,128)(2,1)} %bitcast.7.refs_3_), custom_call_target="tpu_custom_call" | custom-call | tf_op jit(solution)/shard_map/project/pallas_call | solution.py:115
  51.3 6.7 %collective-permute-done.2 = bf16[64,3584]{1,0:T(8,128)(2,1)S(1)} collective-permute-done((bf16[64,3584]{1,0:T(8,128)(2,1)S(1)}, bf16[64,3584]{1,0:T(8,128)(2,1)S(1)}, u32[]{:S(2)}, u32[]{:S(2)}) %collective-permute-start.2) | collective-permute-done | bytes 458784 | tf_op jit(solution)/shard_map/ppermute | solution.py:42
  60.1 4.1 %collective-permute-done.3 = bf16[32,3584]{1,0:T(8,128)(2,1)S(1)} collective-permute-done((bf16[32,3584]{1,0:T(8,128)(2,1)S(1)}, bf16[32,3584]{1,0:T(8,128)(2,1)S(1)}, u32[]{:S(2)}, u32[]{:S(2)}) %collective-permute-start.3) | collective-permute-done | bytes 229408 | tf_op jit(solution)/shard_map/ppermute | solution.py:42
  64.4 2.9 %collective-permute-done.7 = bf16[32,3584]{1,0:T(8,128)(2,1)S(1)} collective-permute-done((bf16[32,3584]{1,0:T(8,128)(2,1)S(1)}, bf16[32,3584]{1,0:T(8,128)(2,1)S(1)}, u32[]{:S(2)}, u32[]{:S(2)}) %collective-permute-start.7) | collective-permute-done | bytes 229408 | tf_op jit(solution)/shard_map/ppermute | solution.py:42
  70.6 3.0 %collective-permute-done.8 = bf16[16,3584]{1,0:T(8,128)(2,1)S(1)} collective-permute-done((bf16[16,3584]{1,0:T(8,128)(2,1)S(1)}, bf16[16,3584]{1,0:T(8,128)(2,1)S(1)}, u32[]{:S(2)}, u32[]{:S(2)}) %collective-permute-start.8) | collective-permute-done | bytes 114720 | tf_op jit(solution)/shard_map/ppermute | solution.py:42
  74.8 3.1 %collective-permute-done.9 = bf16[8,3584]{1,0:T(8,128)(2,1)S(1)} collective-permute-done((bf16[8,3584]{1,0:T(8,128)(2,1)S(1)}, bf16[8,3584]{1,0:T(8,128)(2,1)S(1)}, u32[]{:S(2)}, u32[]{:S(2)}) %collective-permute-start.9) | collective-permute-done | bytes 57376 | tf_op jit(solution)/shard_map/ppermute | solution.py:42
  78.8 1.9 collective-permute-start.10
  81.3 2.6 collective-permute-done.10
  83.9 4.6 %collective-permute-start.14 = (bf16[16,7296]{1,0:T(8,128)(2,1)S(1)}, bf16[16,7296]{1,0:T(8,128)(2,1)S(1)}, u32[]{:S(2)}, u32[]{:S(2)}) collective-permute-start(bf16[16,7296]{1,0:T(8,128)(2,1)S(1)} %pad_maximum_fusion.5), channel_id=1, source_target_pairs={{0,96},{1,33},{2,98},{3,35},{4,100},{5,37},{6,102},{7,39},{8,104},... | collective-permute-start | bytes 700424 | tf_op jit(solution)/shard_map/ppermute | solution.py:42
  89.2 7.9 %collective-permute-done.11 = bf16[16,7296]{1,0:T(8,128)(2,1)S(1)} collective-permute-done((bf16[16,7296]{1,0:T(8,128)(2,1)S(1)}, bf16[16,7296]{1,0:T(8,128)(2,1)S(1)}, u32[]{:S(2)}, u32[]{:S(2)}) %collective-permute-start.11) | collective-permute-done | bytes 233504 | tf_op jit(solution)/shard_map/ppermute | solution.py:42
  98.4 6.3 %collective-permute-done.15 = bf16[16,7296]{1,0:T(8,128)(2,1)S(1)} collective-permute-done((bf16[16,7296]{1,0:T(8,128)(2,1)S(1)}, bf16[16,7296]{1,0:T(8,128)(2,1)S(1)}, u32[]{:S(2)}, u32[]{:S(2)}) %collective-permute-start.15) | collective-permute-done | bytes 233504 | tf_op jit(solution)/shard_map/ppermute | solution.py:42
  108.0 9.1 %collective-permute-done.16 = bf16[32,7296]{1,0:T(8,128)(2,1)S(1)} collective-permute-done((bf16[32,7296]{1,0:T(8,128)(2,1)S(1)}, bf16[32,7296]{1,0:T(8,128)(2,1)S(1)}, u32[]{:S(2)}, u32[]{:S(2)}) %collective-permute-start.16) | collective-permute-done | bytes 466976 | tf_op jit(solution)/shard_map/ppermute | solution.py:42
  117.6 5.2 %collective-permute-done.13 = bf16[64,7296]{1,0:T(8,128)(2,1)S(1)} collective-permute-done((bf16[64,7296]{1,0:T(8,128)(2,1)S(1)}, bf16[64,7296]{1,0:T(8,128)(2,1)S(1)}, u32[]{:S(2)}, u32[]{:S(2)}) %collective-permute-start.13) | collective-permute-done | bytes 933920 | tf_op jit(solution)/shard_map/ppermute | solution.py:42
  125.4 15.4 %collective-permute-done.17 = bf16[64,7296]{1,0:T(8,128)(2,1)S(1)} collective-permute-done((bf16[64,7296]{1,0:T(8,128)(2,1)S(1)}, bf16[64,7296]{1,0:T(8,128)(2,1)S(1)}, u32[]{:S(2)}, u32[]{:S(2)}) %collective-permute-start.17) | collective-permute-done | bytes 933920 | tf_op jit(solution)/shard_map/ppermute | solution.py:42
  142.3 6.6 %collective-permute-done.21.refs_1_.refs_3_ = bf16[128,7296]{1,0:T(8,128)(2,1)} collective-permute-done((bf16[128,7296]{1,0:T(8,128)(2,1)}, bf16[128,7296]{1,0:T(8,128)(2,1)}, u32[]{:S(2)}, u32[]{:S(2)}) %collective-permute-start.21) | collective-permute-done | bytes 1867808 | tf_op jit(solution)/shard_map/ppermute | solution.py:42
  149.0 17.2 %collective-permute-done.22.refs_2_.refs_4_ = bf16[128,7296]{1,0:T(8,128)(2,1)} collective-permute-done((bf16[128,7296]{1,0:T(8,128)(2,1)S(1)}, bf16[128,7296]{1,0:T(8,128)(2,1)}, u32[]{:S(2)}, u32[]{:S(2)}) %collective-permute-start.22) | collective-permute-done | bytes 1867808 | tf_op jit(solution)/shard_map/ppermute | solution.py:42
  166.1 18.7 %experts.3 = (bf16[128,7168]{1,0:T(8,128)(2,1)}, bf16[128,7168]{1,0:T(8,128)(2,1)}) custom-call(s32[2]{0:T(128)} %pad_add_fusion.refs_0_, bf16[128,7296]{1,0:T(8,128)(2,1)} %collective-permute-done.21.refs_1_.refs_3_, bf16[128,7296]{1,0:T(8,128)(2,1)} %collective-permute-done.22.refs_2_.refs_4_, bf16[128,7296]{1,0:T(8,128)(2,1)} %collective-permute-done.21.refs_1_.refs_3_, ...), custom_call_target="tpu_custom_call" | custom-call | tf_op jit(solution)/shard_map/experts/pallas_call | solution.py:187
  187.1 18.5 %experts.2 = (bf16[128,7168]{1,0:T(8,128)(2,1)}, bf16[128,7168]{1,0:T(8,128)(2,1)}) custom-call(s32[2]{0:T(128)} %pad_add_fusion.refs_0_, bf16[128,7296]{1,0:T(8,128)(2,1)} %constant_dynamic-update-slice_fusion.refs_1_.refs_3_, bf16[128,7296]{1,0:T(8,128)(2,1)} %copy-done, bf16[128,7296]{1,0:T(8,128)(2,1)} %constant_dynamic-update-slice_fusion.refs_1_.refs_3_, ...), custom_call_target="tpu_custom_call" | custom-call | tf_op jit(solution)/shard_map/experts/pallas_call | solution.py:187
  205.7 13.8 %collective-permute-done.27 = bf16[128,7168]{1,0:T(8,128)(2,1)} collective-permute-done((bf16[128,7168]{1,0:T(8,128)(2,1)}, bf16[128,7168]{1,0:T(8,128)(2,1)}, u32[]{:S(2)}, u32[]{:S(2)}) %collective-permute-start.27) | collective-permute-done | bytes 1835040 | tf_op jit(solution)/shard_map/ppermute | solution.py:42
  219.5 2.5 add_convert_fusion
  224.1 13.4 %collective-permute-done.28 = bf16[64,7168]{1,0:T(8,128)(2,1)S(1)} collective-permute-done((bf16[64,7168]{1,0:T(8,128)(2,1)S(1)}, bf16[64,7168]{1,0:T(8,128)(2,1)S(1)}, u32[]{:S(2)}, u32[]{:S(2)}) %collective-permute-start.28) | collective-permute-done | bytes 917536 | tf_op jit(solution)/shard_map/ppermute | solution.py:42
  237.7 1.9 collective-permute-start.29
  239.9 1.9 collective-permute-start.25
  241.8 5.7 %collective-permute-done.29 = bf16[32,7168]{1,0:T(8,128)(2,1)S(1)} collective-permute-done((bf16[32,7168]{1,0:T(8,128)(2,1)S(1)}, bf16[32,7168]{1,0:T(8,128)(2,1)S(1)}, u32[]{:S(2)}, u32[]{:S(2)}) %collective-permute-start.29) | collective-permute-done | bytes 458784 | tf_op jit(solution)/shard_map/ppermute | solution.py:42
  247.7 1.9 collective-permute-done.25
  249.9 3.8 %collective-permute-done.30 = bf16[16,7168]{1,0:T(8,128)(2,1)S(1)} collective-permute-done((bf16[16,7168]{1,0:T(8,128)(2,1)S(1)}, bf16[16,7168]{1,0:T(8,128)(2,1)S(1)}, u32[]{:S(2)}, u32[]{:S(2)}) %collective-permute-start.30) | collective-permute-done | bytes 229408 | tf_op jit(solution)/shard_map/ppermute | solution.py:42
  253.9 2.0 collective-permute-done.26
  255.9 5.2 %collective-permute-done.31 = bf16[16,7168]{1,0:T(8,128)(2,1)S(1)} collective-permute-done((bf16[16,7168]{1,0:T(8,128)(2,1)S(1)}, bf16[16,7168]{1,0:T(8,128)(2,1)S(1)}, u32[]{:S(2)}, u32[]{:S(2)}) %collective-permute-start.31) | collective-permute-done | bytes 229408 | tf_op jit(solution)/shard_map/ppermute | solution.py:42
  261.3 4.8 %collective-permute-done.32 = bf16[8,7168]{1,0:T(8,128)(2,1)S(1)} collective-permute-done((bf16[8,7168]{1,0:T(8,128)(2,1)S(1)}, bf16[8,7168]{1,0:T(8,128)(2,1)S(1)}, u32[]{:S(2)}, u32[]{:S(2)}) %collective-permute-start.32) | collective-permute-done | bytes 114720 | tf_op jit(solution)/shard_map/ppermute | solution.py:42
  (117 shorter events, 32.1 us)
Async XLA Ops:
  0.0 37.1 %collective-permute-start.1 = (bf16[4,128,7168]{2,1,0:T(8,128)(2,1)}, bf16[4,128,7168]{2,1,0:T(8,128)(2,1)}, u32[]{:S(2)}, u32[]{:S(2)}) collective-permute-start(bf16[4,128,7168]{2,1,0:T(8,128)(2,1)} %param.16), channel_id=1, source_target_pairs={{0,1},{1,0},{2,3},{3,2},{4,5},{5,4},{6,7},{7,6},{8,9},{9,8},{10,11... | collective-permute-start | bytes 22020104 | tf_op jit(solution)/shard_map/ppermute | solution.py:46
  8.0 25.9 %all-to-all-start = ((bf16[16,8,8,512]{3,2,1,0:T(8,128)(2,1)}), bf16[16,8,8,512]{3,2,1,0:T(8,128)(2,1)S(1)}, u32[]{:S(2)}, u32[]{:S(2)}) async-start(bf16[16,8,8,512]{3,2,1,0:T(8,128)(2,1)} %attend.1), calls=%async_computation | async-start | bytes 2097152 | tf_op jit(solution)/shard_map/all_to_all | solution.py:273
  15.5 19.3 %collective-permute-start = (bf16[4,512,128]{1,2,0:T(8,128)(2,1)S(1)}, bf16[4,512,128]{1,2,0:T(8,128)(2,1)S(1)}, u32[]{:S(2)}, u32[]{:S(2)}) collective-permute-start(bf16[4,512,128]{1,2,0:T(8,128)(2,1)S(1)} %copy.15), channel_id=1, source_target_pairs={{0,1},{1,0},{2,3},{3,2},{4,5},{5,4},{6,7},{7,6},{8,9},{9,8},{10,11... | collective-permute-start | bytes 1572872 | tf_op jit(solution)/shard_map/ppermute | solution.py:46
  48.3 9.8 %collective-permute-start.2 = (bf16[64,3584]{1,0:T(8,128)(2,1)S(1)}, bf16[64,3584]{1,0:T(8,128)(2,1)S(1)}, u32[]{:S(2)}, u32[]{:S(2)}) collective-permute-start(bf16[64,3584]{1,0:T(8,128)(2,1)S(1)} %slice.91), channel_id=1, source_target_pairs={{0,24},{1,9},{2,26},{3,11},{4,28},{5,13},{6,30},{7,15},{8,16},{9,1... | collective-permute-start | bytes 1376264 | tf_op jit(solution)/shard_map/ppermute | solution.py:42
  50.1 9.8 %collective-permute-start.6 = (bf16[64,3584]{1,0:T(8,128)(2,1)S(1)}, bf16[64,3584]{1,0:T(8,128)(2,1)S(1)}, u32[]{:S(2)}, u32[]{:S(2)}) collective-permute-start(bf16[64,3584]{1,0:T(8,128)(2,1)S(1)} %slice.99), channel_id=1, source_target_pairs={{0,6},{1,3},{2,4},{3,1},{4,2},{5,7},{6,0},{7,5},{8,14},{9,11},{10,... | collective-permute-start | bytes 1376264 | tf_op jit(solution)/shard_map/ppermute | solution.py:42
  58.2 6.1 %collective-permute-start.3 = (bf16[32,3584]{1,0:T(8,128)(2,1)S(1)}, bf16[32,3584]{1,0:T(8,128)(2,1)S(1)}, u32[]{:S(2)}, u32[]{:S(2)}) collective-permute-start(bf16[32,3584]{1,0:T(8,128)(2,1)S(1)} %slice.121), channel_id=1, source_target_pairs={{0,8},{1,25},{2,10},{3,27},{4,12},{5,29},{6,14},{7,31},{8,0},{9,17... | collective-permute-start | bytes 688136 | tf_op jit(solution)/shard_map/ppermute | solution.py:42
  60.0 7.3 %collective-permute-start.7 = (bf16[32,3584]{1,0:T(8,128)(2,1)S(1)}, bf16[32,3584]{1,0:T(8,128)(2,1)S(1)}, u32[]{:S(2)}, u32[]{:S(2)}) collective-permute-start(bf16[32,3584]{1,0:T(8,128)(2,1)S(1)} %slice.127), channel_id=1, source_target_pairs={{0,2},{1,7},{2,0},{3,5},{4,6},{5,3},{6,4},{7,1},{8,10},{9,15},{10,... | collective-permute-start | bytes 688136 | tf_op jit(solution)/shard_map/ppermute | solution.py:42
  64.3 6.1 %collective-permute-start.4 = (bf16[16,3584]{1,0:T(8,128)(2,1)S(1)}, bf16[16,3584]{1,0:T(8,128)(2,1)S(1)}, u32[]{:S(2)}, u32[]{:S(2)}) collective-permute-start(bf16[16,3584]{1,0:T(8,128)(2,1)S(1)} %slice.123), channel_id=1, source_target_pairs={{0,6},{1,3},{2,4},{3,1},{4,2},{5,7},{6,0},{7,5},{8,14},{9,11},{10,... | collective-permute-start | bytes 344072 | tf_op jit(solution)/shard_map/ppermute | solution.py:42
  67.4 6.1 %collective-permute-start.8 = (bf16[16,3584]{1,0:T(8,128)(2,1)S(1)}, bf16[16,3584]{1,0:T(8,128)(2,1)S(1)}, u32[]{:S(2)}, u32[]{:S(2)}) collective-permute-start(bf16[16,3584]{1,0:T(8,128)(2,1)S(1)} %slice.129), channel_id=1, source_target_pairs={{0,24},{1,9},{2,26},{3,11},{4,28},{5,13},{6,30},{7,15},{8,16},{9,1... | collective-permute-start | bytes 344072 | tf_op jit(solution)/shard_map/ppermute | solution.py:42
  78.8 5.1 %collective-permute-start.10 = (bf16[8,7296]{1,0:T(8,128)(2,1)S(1)}, bf16[8,7296]{1,0:T(8,128)(2,1)S(1)}, u32[]{:S(2)}, u32[]{:S(2)}) collective-permute-start(bf16[8,7296]{1,0:T(8,128)(2,1)S(1)} %get-tuple-element.19), channel_id=1, source_target_pairs={{0,32},{1,97},{2,34},{3,99},{4,36},{5,101},{6,38},{7,103},{8,40},{... | collective-permute-start | bytes 350216 | tf_op jit(solution)/shard_map/ppermute | solution.py:42
  80.8 61.6 %collective-permute-start.18 = (bf16[1,7168,256]{2,1,0:T(8,128)(2,1)}, bf16[1,7168,256]{2,1,0:T(8,128)(2,1)}, u32[]{:S(2)}, u32[]{:S(2)}) collective-permute-start(bf16[1,7168,256]{2,1,0:T(8,128)(2,1)} %refs_5_.3), channel_id=1, source_target_pairs={{0,1},{1,0},{2,3},{3,2},{4,5},{5,4},{6,7},{7,6},{8,9},{9,8},{10,11... | collective-permute-start | bytes 11010056 | tf_op jit(solution)/shard_map/ppermute | solution.py:46
  80.8 61.6 %collective-permute-start.19 = (bf16[1,7168,256]{2,1,0:T(8,128)(2,1)}, bf16[1,7168,256]{2,1,0:T(8,128)(2,1)}, u32[]{:S(2)}, u32[]{:S(2)}) collective-permute-start(bf16[1,7168,256]{2,1,0:T(8,128)(2,1)} %refs_7_.3), channel_id=1, source_target_pairs={{0,1},{1,0},{2,3},{3,2},{4,5},{5,4},{6,7},{7,6},{8,9},{9,8},{10,11... | collective-permute-start | bytes 11010056 | tf_op jit(solution)/shard_map/ppermute | solution.py:46
  81.3 61.1 %collective-permute-start.20 = (bf16[1,256,7168]{2,1,0:T(8,128)(2,1)}, bf16[1,256,7168]{2,1,0:T(8,128)(2,1)}, u32[]{:S(2)}, u32[]{:S(2)}) collective-permute-start(bf16[1,256,7168]{2,1,0:T(8,128)(2,1)} %refs_9_.3), channel_id=1, source_target_pairs={{0,1},{1,0},{2,3},{3,2},{4,5},{5,4},{6,7},{7,6},{8,9},{9,8},{10,11... | collective-permute-start | bytes 11010056 | tf_op jit(solution)/shard_map/ppermute | solution.py:46
  83.9 13.7 %collective-permute-start.14 = (bf16[16,7296]{1,0:T(8,128)(2,1)S(1)}, bf16[16,7296]{1,0:T(8,128)(2,1)S(1)}, u32[]{:S(2)}, u32[]{:S(2)}) collective-permute-start(bf16[16,7296]{1,0:T(8,128)(2,1)S(1)} %pad_maximum_fusion.5), channel_id=1, source_target_pairs={{0,96},{1,33},{2,98},{3,35},{4,100},{5,37},{6,102},{7,39},{8,104},... | collective-permute-start | bytes 700424 | tf_op jit(solution)/shard_map/ppermute | solution.py:42
  88.5 8.6 %collective-permute-start.11 = (bf16[16,7296]{1,0:T(8,128)(2,1)S(1)}, bf16[16,7296]{1,0:T(8,128)(2,1)S(1)}, u32[]{:S(2)}, u32[]{:S(2)}) collective-permute-start(bf16[16,7296]{1,0:T(8,128)(2,1)S(1)} %pad_maximum_fusion.5), channel_id=1, source_target_pairs={{0,2},{1,7},{2,0},{3,5},{4,6},{5,3},{6,4},{7,1},{8,10},{9,15},{10,... | collective-permute-start | bytes 700424 | tf_op jit(solution)/shard_map/ppermute | solution.py:42
  97.1 9.9 %collective-permute-start.12 = (bf16[32,7296]{1,0:T(8,128)(2,1)S(1)}, bf16[32,7296]{1,0:T(8,128)(2,1)S(1)}, u32[]{:S(2)}, u32[]{:S(2)}) collective-permute-start(bf16[32,7296]{1,0:T(8,128)(2,1)S(1)} %pad_maximum_fusion.2), channel_id=1, source_target_pairs={{0,6},{1,3},{2,4},{3,1},{4,2},{5,7},{6,0},{7,5},{8,14},{9,11},{10,... | collective-permute-start | bytes 1400840 | tf_op jit(solution)/shard_map/ppermute | solution.py:42
  97.6 7.0 %collective-permute-start.15 = (bf16[16,7296]{1,0:T(8,128)(2,1)S(1)}, bf16[16,7296]{1,0:T(8,128)(2,1)S(1)}, u32[]{:S(2)}, u32[]{:S(2)}) collective-permute-start(bf16[16,7296]{1,0:T(8,128)(2,1)S(1)} %collective-permute-done.14), channel_id=1, source_target_pairs={{0,8},{1,25},{2,10},{3,27},{4,12},{5,29},{6,14},{7,31},{8,0},{9,17... | collective-permute-start | bytes 700424 | tf_op jit(solution)/shard_map/ppermute | solution.py:42
  104.7 12.4 %collective-permute-start.16 = (bf16[32,7296]{1,0:T(8,128)(2,1)S(1)}, bf16[32,7296]{1,0:T(8,128)(2,1)S(1)}, u32[]{:S(2)}, u32[]{:S(2)}) collective-permute-start(bf16[32,7296]{1,0:T(8,128)(2,1)S(1)} %pad_maximum_fusion.3), channel_id=1, source_target_pairs={{0,24},{1,9},{2,26},{3,11},{4,28},{5,13},{6,30},{7,15},{8,16},{9,1... | collective-permute-start | bytes 1400840 | tf_op jit(solution)/shard_map/ppermute | solution.py:42
  107.1 15.8 %collective-permute-start.13 = (bf16[64,7296]{1,0:T(8,128)(2,1)S(1)}, bf16[64,7296]{1,0:T(8,128)(2,1)S(1)}, u32[]{:S(2)}, u32[]{:S(2)}) collective-permute-start(bf16[64,7296]{1,0:T(8,128)(2,1)S(1)} %pad_maximum_fusion), channel_id=1, source_target_pairs={{0,8},{1,25},{2,10},{3,27},{4,12},{5,29},{6,14},{7,31},{8,0},{9,17... | collective-permute-start | bytes 2801672 | tf_op jit(solution)/shard_map/ppermute | solution.py:42
  117.2 23.7 %collective-permute-start.17 = (bf16[64,7296]{1,0:T(8,128)(2,1)S(1)}, bf16[64,7296]{1,0:T(8,128)(2,1)S(1)}, u32[]{:S(2)}, u32[]{:S(2)}) collective-permute-start(bf16[64,7296]{1,0:T(8,128)(2,1)S(1)} %pad_maximum_fusion.1), channel_id=1, source_target_pairs={{0,2},{1,7},{2,0},{3,5},{4,6},{5,3},{6,4},{7,1},{8,10},{9,15},{10,... | collective-permute-start | bytes 2801672 | tf_op jit(solution)/shard_map/ppermute | solution.py:42
  123.9 25.1 %collective-permute-start.21 = (bf16[128,7296]{1,0:T(8,128)(2,1)}, bf16[128,7296]{1,0:T(8,128)(2,1)}, u32[]{:S(2)}, u32[]{:S(2)}) collective-permute-start(bf16[128,7296]{1,0:T(8,128)(2,1)} %constant_dynamic-update-slice_fusion.refs_1_.refs_3_), channel_id=1, source_target_pairs={{0,24},{1,9},{2,26},{3,11},{4,28},{5,13},{6,30},{7,15},{8,16},{9,1... | collective-permute-start | bytes 5603336 | tf_op jit(solution)/shard_map/ppermute | solution.py:42
  141.0 25.2 %collective-permute-start.22 = (bf16[128,7296]{1,0:T(8,128)(2,1)S(1)}, bf16[128,7296]{1,0:T(8,128)(2,1)}, u32[]{:S(2)}, u32[]{:S(2)}) collective-permute-start(bf16[128,7296]{1,0:T(8,128)(2,1)S(1)} %constant_dynamic-update-slice_fusion.5.refs_2_.refs_4_), channel_id=1, source_target_pairs={{0,6},{1,3},{2,4},{3,1},{4,2},{5,7},{6,0},{7,5},{8,14},{9,11},{10,... | collective-permute-start | bytes 5603336 | tf_op jit(solution)/shard_map/ppermute | solution.py:42
  184.8 34.7 %collective-permute-start.27 = (bf16[128,7168]{1,0:T(8,128)(2,1)}, bf16[128,7168]{1,0:T(8,128)(2,1)}, u32[]{:S(2)}, u32[]{:S(2)}) collective-permute-start(bf16[128,7168]{1,0:T(8,128)(2,1)} %get-tuple-element.16), channel_id=1, source_target_pairs={{0,6},{1,3},{2,4},{3,1},{4,2},{5,7},{6,0},{7,5},{8,14},{9,11},{10,... | collective-permute-start | bytes 5505032 | tf_op jit(solution)/shard_map/ppermute | solution.py:42
  185.3 36.8 %collective-permute-start.23 = (bf16[128,7168]{1,0:T(8,128)(2,1)}, bf16[128,7168]{1,0:T(8,128)(2,1)S(1)}, u32[]{:S(2)}, u32[]{:S(2)}) collective-permute-start(bf16[128,7168]{1,0:T(8,128)(2,1)} %get-tuple-element.14), channel_id=1, source_target_pairs={{0,24},{1,9},{2,26},{3,11},{4,28},{5,13},{6,30},{7,15},{8,16},{9,1... | collective-permute-start | bytes 5505032 | tf_op jit(solution)/shard_map/ppermute | solution.py:42
  222.1 15.4 %collective-permute-start.28 = (bf16[64,7168]{1,0:T(8,128)(2,1)S(1)}, bf16[64,7168]{1,0:T(8,128)(2,1)S(1)}, u32[]{:S(2)}, u32[]{:S(2)}) collective-permute-start(bf16[64,7168]{1,0:T(8,128)(2,1)S(1)} %slice.139), channel_id=1, source_target_pairs={{0,2},{1,7},{2,0},{3,5},{4,6},{5,3},{6,4},{7,1},{8,10},{9,15},{10,... | collective-permute-start | bytes 2752520 | tf_op jit(solution)/shard_map/ppermute | solution.py:42
  224.0 15.6 %collective-permute-start.24 = (bf16[64,7168]{1,0:T(8,128)(2,1)S(1)}, bf16[64,7168]{1,0:T(8,128)(2,1)S(1)}, u32[]{:S(2)}, u32[]{:S(2)}) collective-permute-start(bf16[64,7168]{1,0:T(8,128)(2,1)S(1)} %slice.133), channel_id=1, source_target_pairs={{0,8},{1,25},{2,10},{3,27},{4,12},{5,29},{6,14},{7,31},{8,0},{9,17... | collective-permute-start | bytes 2752520 | tf_op jit(solution)/shard_map/ppermute | solution.py:42
  237.7 9.8 %collective-permute-start.29 = (bf16[32,7168]{1,0:T(8,128)(2,1)S(1)}, bf16[32,7168]{1,0:T(8,128)(2,1)S(1)}, u32[]{:S(2)}, u32[]{:S(2)}) collective-permute-start(bf16[32,7168]{1,0:T(8,128)(2,1)S(1)} %slice.141), channel_id=1, source_target_pairs={{0,24},{1,9},{2,26},{3,11},{4,28},{5,13},{6,30},{7,15},{8,16},{9,1... | collective-permute-start | bytes 1376264 | tf_op jit(solution)/shard_map/ppermute | solution.py:42
  239.9 9.8 %collective-permute-start.25 = (bf16[32,7168]{1,0:T(8,128)(2,1)S(1)}, bf16[32,7168]{1,0:T(8,128)(2,1)S(1)}, u32[]{:S(2)}, u32[]{:S(2)}) collective-permute-start(bf16[32,7168]{1,0:T(8,128)(2,1)S(1)} %slice.135), channel_id=1, source_target_pairs={{0,6},{1,3},{2,4},{3,1},{4,2},{5,7},{6,0},{7,5},{8,14},{9,11},{10,... | collective-permute-start | bytes 1376264 | tf_op jit(solution)/shard_map/ppermute | solution.py:42
  247.6 6.1 %collective-permute-start.30 = (bf16[16,7168]{1,0:T(8,128)(2,1)S(1)}, bf16[16,7168]{1,0:T(8,128)(2,1)S(1)}, u32[]{:S(2)}, u32[]{:S(2)}) collective-permute-start(bf16[16,7168]{1,0:T(8,128)(2,1)S(1)} %slice.143), channel_id=1, source_target_pairs={{0,8},{1,25},{2,10},{3,27},{4,12},{5,29},{6,14},{7,31},{8,0},{9,17... | collective-permute-start | bytes 688136 | tf_op jit(solution)/shard_map/ppermute | solution.py:42
  249.8 6.1 %collective-permute-start.26 = (bf16[16,7168]{1,0:T(8,128)(2,1)S(1)}, bf16[16,7168]{1,0:T(8,128)(2,1)S(1)}, u32[]{:S(2)}, u32[]{:S(2)}) collective-permute-start(bf16[16,7168]{1,0:T(8,128)(2,1)S(1)} %slice.137), channel_id=1, source_target_pairs={{0,2},{1,7},{2,0},{3,5},{4,6},{5,3},{6,4},{7,1},{8,10},{9,15},{10,... | collective-permute-start | bytes 688136 | tf_op jit(solution)/shard_map/ppermute | solution.py:42
  253.8 7.3 %collective-permute-start.31 = (bf16[16,7168]{1,0:T(8,128)(2,1)S(1)}, bf16[16,7168]{1,0:T(8,128)(2,1)S(1)}, u32[]{:S(2)}, u32[]{:S(2)}) collective-permute-start(bf16[16,7168]{1,0:T(8,128)(2,1)S(1)} %add_convert_fusion.9), channel_id=1, source_target_pairs={{0,96},{1,33},{2,98},{3,35},{4,100},{5,37},{6,102},{7,39},{8,104},... | collective-permute-start | bytes 688136 | tf_op jit(solution)/shard_map/ppermute | solution.py:42
  261.2 4.9 %collective-permute-start.32 = (bf16[8,7168]{1,0:T(8,128)(2,1)S(1)}, bf16[8,7168]{1,0:T(8,128)(2,1)S(1)}, u32[]{:S(2)}, u32[]{:S(2)}) collective-permute-start(bf16[8,7168]{1,0:T(8,128)(2,1)S(1)} %slice.145), channel_id=1, source_target_pairs={{0,32},{1,97},{2,34},{3,99},{4,36},{5,101},{6,38},{7,103},{8,40},{... | collective-permute-start | bytes 344072 | tf_op jit(solution)/shard_map/ppermute | solution.py:42
  (10 other events, 126.5 us)
where the time goes:
time: 268 us; the launch traced here: 267 us
  waiting for transfers between devices  163 us (61%)
  Pallas kernels  55.1 us (21%)
  starting transfers between devices  30.4 us (11%)
  local copies, waits for them, and re-layouts  8.01 us (3%)
  other arithmetic  6.8 us (3%)
    ppermute x28, waiting for transfers between devices, swap(): return lax.ppermute(value, ALL, ring_pairs(axis, step))  145 us
    pallas_call x2, Pallas kernels, experts(): pl.pallas_call(lambda *refs: experts_kernel(steps, *refs), grid_spec=pltp...  37.2 us
    ppermute x28, starting transfers between devices, swap(): return lax.ppermute(value, ALL, ring_pairs(axis, step))  22.3 us
    all_to_all x1, waiting for transfers between devices, run_rows(): lax.all_to_all(heads_out, 'dev', split_axis=0, concat_axis=0, tiled=True,...  18.1 us
    pallas_call x1, Pallas kernels, project(): pl.pallas_call(lambda *refs: project_kernel(steps, *refs), grid=(2 * step...  9.95 us
    pallas_call x1, Pallas kernels, attend(): pl.pallas_call(attend_kernel, grid_spec=pltpu.PrefetchScalarGridSpec(num_...  7.98 us
    all_to_all x1, starting transfers between devices, run_rows(): lax.all_to_all(heads_out, 'dev', split_axis=0, concat_axis=0, tiled=True,...  7.27 us
  transfers between devices with their start and end apart: 34, of which 26 were waited for; matrix products, arithmetic and copies ran while one was open for 5% of the time, Pallas kernels for 10%

commit v1 on v0

--- a/solution.py
+++ b/solution.py
@@ -35,11 +35,24 @@
     return pairs
 
 
+def ring_next(axis):
+    pairs = []
+    for i in range(128):
+        at = place(i)
+        at[axis] = (at[axis] + (1 if at[3] == 0 else 3)) % 4
+        pairs.append((i, number(at)))
+    return pairs
+
+
 Z, Y, X = 0, 1, 2
 
 
 def swap(value, axis, step):
     return lax.ppermute(value, ALL, ring_pairs(axis, step))
+
+
+def onward(value, axis):
+    return lax.ppermute(value, ALL, ring_next(axis))
 
 
 def other_core(value):
@@ -107,7 +120,7 @@
 def project(left_in, right_in, own, other):
     rows, depth = left_in.shape
     width = own.shape[1]
-    block = 896
+    block = 1792
     steps = width // 2 // block
     whole = pl.BlockSpec((rows, depth), lambda i: (0, 0))
     matrix = pl.BlockSpec((depth // 2, block), lambda i: (0, i))
@@ -125,7 +138,7 @@
     )(left_in, right_in, own, other)
 
 
-BLOCK = 1024
+BLOCK = 1792
 
 
 def experts_kernel(
@@ -308,26 +321,33 @@
     routing = jnp.pad(routing, ((0, 0), (0, 128 - routing.shape[1])))
     first = grow(jnp.concatenate([normed, routing], axis=1), Z, 0)
     second = swap(first, Z, 1)
-    for axis_first, axis_second, step in ((X, Y, 0), (X, Y, 1), (Y, X, 0)):
-        first = grow(first, axis_first, step)
-        second = grow(second, axis_second, step)
-    first_far = swap(first, Y, 1)
-    second_far = swap(second, X, 1)
+    for step in range(2):
+        first = grow(first, X, step)
+        second = grow(second, Y, step)
+
+    def add(one, two):
+        return (one.astype(F32) + two.astype(F32)).astype(BF)
 
     numbers = jnp.stack([device, device ^ 1]).astype(jnp.int32)
     weights = (w_gate, gate_other, w_up, up_other, w_down, down_other)
-    out_first, out_second = experts(numbers, first, second, weights, width)
-    out_first_far, out_second_far = experts(numbers, first_far, second_far, weights, width)
-
-    def add(one, two):
-        return (one.astype(F32) + two.astype(F32)).astype(BF)
-
-    out_first = add(out_first, swap(out_first_far, Y, 1))
-    out_second = add(out_second, swap(out_second_far, X, 1))
-    for axis_first, axis_second, step in ((Y, X, 0), (X, Y, 1), (X, Y, 0)):
-        out_first = fold(out_first, axis_first, step)
-        out_second = fold(out_second, axis_second, step)
-    combined = add(out_first, swap(out_second, Z, 1))
+    held = [(first, second)]
+    for _ in range(1, 4):
+        one = onward(held[-1][0], Y)
+        two = onward(held[-1][1], X)
+        held.append((one, two))
+    done = []
+    for hop in range(4):
+        done.append(experts(numbers, *held[hop], weights, width))
+    one, two = done[1]
+    for hop in range(1, 4):
+        one = onward(one, Y)
+        two = onward(two, X)
+        one = add(one, done[(hop + 1) % 4][0])
+        two = add(two, done[(hop + 1) % 4][1])
+    for step in (1, 0):
+        one = fold(one, X, step)
+        two = fold(two, Y, step)
+    combined = add(one, swap(two, Z, 1))
     keep, send = halves(combined)
     combined = keep.astype(F32) + swap(send, Z, 0).astype(F32)
     return (residual + combined).astype(BF)
@@ -348,4 +368,6 @@
         P("dev", None, "grp"),
         P("dev", "grp", None),
     )
-    return jax.shard_map(run_rows, mesh=mesh, in_specs=in_specs, out_specs=both, check_vma=False)
+    return jax.shard_map(
+        run_rows, mesh=mesh, in_specs=in_specs, out_specs=both, check_vma=False
+    )

time: 268 us -> 263 us (0.981)
  the two profiles are of different devices: /device:TPU:0 before, /device:TPU:10 now
where the time goes in v1:
time: 263 us; the launch traced here: 262 us
  waiting for transfers between devices  109 us (41%)
  Pallas kernels  71.9 us (27%)
  starting transfers between devices  62.8 us (24%)
  other arithmetic  11 us (4%)
  local copies, waits for them, and re-layouts  4.25 us (2%)
  matrix products  2.63 us (1%)
    pallas_call x4, Pallas kernels, experts(): pl.pallas_call(lambda *refs: experts_kernel(steps, *refs), grid_spec=pltp...  55.9 us
    ppermute x20, waiting for transfers between devices, swap(): return lax.ppermute(value, ALL, ring_pairs(axis, step))  52.5 us
    ppermute x12, waiting for transfers between devices, onward(): return lax.ppermute(value, ALL, ring_next(axis))  41.8 us
    ppermute x20, starting transfers between devices, swap(): return lax.ppermute(value, ALL, ring_pairs(axis, step))  37.4 us
    ppermute x12, starting transfers between devices, onward(): return lax.ppermute(value, ALL, ring_next(axis))  17.3 us
    all_to_all x1, waiting for transfers between devices, run_rows(): lax.all_to_all(heads_out, 'dev', split_axis=0, concat_axis=0, tiled=True,...  14.5 us
    convert_element_type x7, other arithmetic, add(): return (one.astype(F32) + two.astype(F32)).astype(BF)  8.39 us
    pallas_call x1, Pallas kernels, project(): pl.pallas_call(lambda *refs: project_kernel(steps, *refs), grid=(2 * step...  8.01 us
  transfers between devices with their start and end apart: 38, of which 19 were waited for; matrix products, arithmetic and copies ran while one was open for 6% of the time, Pallas kernels for 24%

profile of v1, /device:TPU:10, one launch (start us, length us, event | category | flops | bytes accessed | tf_op | source)
XLA Modules:
  0.0 261.9 jit_solution(291299121673793720)
XLA Ops:
  0.0 8.0 %attend.1 = bf16[16,8,8,512]{3,2,1,0:T(8,128)(2,1)} custom-call(s32[8]{0:T(128)} %length_ref.1, bf16[8,576,128]{2,1,0:T(8,128)(2,1)} %bitcast.21, bf16[8,576,512]{2,1,0:T(8,128)(2,1)} %bitcast.17), custom_call_target="tpu_custom_call" | custom-call | tf_op jit(solution)/shard_map/attend/pallas_call | solution.py:86
  8.0 7.5 %all-to-all-start = ((bf16[16,8,8,512]{3,2,1,0:T(8,128)(2,1)}), bf16[16,8,8,512]{3,2,1,0:T(8,128)(2,1)S(1)}, u32[]{:S(2)}, u32[]{:S(2)}) async-start(bf16[16,8,8,512]{3,2,1,0:T(8,128)(2,1)} %attend.1), calls=%async_computation | async-start | bytes 2097152 | tf_op jit(solution)/shard_map/all_to_all | solution.py:286
  15.9 14.5 %all-to-all-done = bf16[16,8,8,512]{3,2,1,0:T(8,128)(2,1)S(1)} async-done(((bf16[16,8,8,512]{3,2,1,0:T(8,128)(2,1)}), bf16[16,8,8,512]{3,2,1,0:T(8,128)(2,1)S(1)}, u32[]{:S(2)}, u32[]{:S(2)}) %all-to-all-start) | async-done | bytes 1048608 | tf_op jit(solution)/shard_map/all_to_all | solution.py:286
  33.6 8.0 %project.1 = (bf16[128,3584]{1,0:T(8,128)(2,1)}, bf16[128,3584]{1,0:T(8,128)(2,1)}) custom-call(bf16[128,1024]{1,0:T(8,128)(2,1)} %convolution_convert_fusion.1.refs_0_, bf16[128,1024]{1,0:T(8,128)(2,1)} %convolution_convert_fusion.refs_1_, bf16[512,7168]{1,0:T(8,128)(2,1)} %bitcast.16, bf16[512,7168]{1,0:T(8,128)(2,1)} %bitcast.7.refs_3_), custom_call_target="tpu_custom_call" | custom-call | tf_op jit(solution)/shard_map/project/pallas_call | solution.py:128
  46.6 4.7 %collective-permute-done.2 = bf16[64,3584]{1,0:T(8,128)(2,1)S(1)} collective-permute-done((bf16[64,3584]{1,0:T(8,128)(2,1)S(1)}, bf16[64,3584]{1,0:T(8,128)(2,1)S(1)}, u32[]{:S(2)}, u32[]{:S(2)}) %collective-permute-start.2) | collective-permute-done | bytes 458784 | tf_op jit(solution)/shard_map/ppermute | solution.py:51
  51.5 3.4 %collective-permute-start.3 = (bf16[32,3584]{1,0:T(8,128)(2,1)S(1)}, bf16[32,3584]{1,0:T(8,128)(2,1)S(1)}, u32[]{:S(2)}, u32[]{:S(2)}) collective-permute-start(bf16[32,3584]{1,0:T(8,128)(2,1)S(1)} %slice.105), channel_id=1, source_target_pairs={{0,8},{1,25},{2,10},{3,27},{4,12},{5,29},{6,14},{7,31},{8,0},{9,17... | collective-permute-start | bytes 688136 | tf_op jit(solution)/shard_map/ppermute | solution.py:51
  59.4 2.5 collective-permute-done.7
  64.1 3.4 %collective-permute-start.5 = (bf16[8,3584]{1,0:T(8,128)(2,1)S(1)}, bf16[8,3584]{1,0:T(8,128)(2,1)S(1)}, u32[]{:S(2)}, u32[]{:S(2)}) collective-permute-start(bf16[8,3584]{1,0:T(8,128)(2,1)S(1)} %slice.109), channel_id=1, source_target_pairs={{0,2},{1,7},{2,0},{3,5},{4,6},{5,3},{6,4},{7,1},{8,10},{9,15},{10,... | collective-permute-start | bytes 172040 | tf_op jit(solution)/shard_map/ppermute | solution.py:51
  67.5 3.0 %collective-permute-start.9 = (bf16[8,3584]{1,0:T(8,128)(2,1)S(1)}, bf16[8,3584]{1,0:T(8,128)(2,1)S(1)}, u32[]{:S(2)}, u32[]{:S(2)}) collective-permute-start(bf16[8,3584]{1,0:T(8,128)(2,1)S(1)} %slice.115), channel_id=1, source_target_pairs={{0,8},{1,25},{2,10},{3,27},{4,12},{5,29},{6,14},{7,31},{8,0},{9,17... | collective-permute-start | bytes 172040 | tf_op jit(solution)/shard_map/ppermute | solution.py:51
  75.1 2.9 %collective-permute-done.10 = bf16[8,7296]{1,0:T(8,128)(2,1)S(1)} collective-permute-done((bf16[8,7296]{1,0:T(8,128)(2,1)S(1)}, bf16[8,7296]{1,0:T(8,128)(2,1)S(1)}, u32[]{:S(2)}, u32[]{:S(2)}) %collective-permute-start.10) | collective-permute-done | bytes 116768 | tf_op jit(solution)/shard_map/ppermute | solution.py:51
  80.6 4.0 %collective-permute-start.14 = (bf16[16,7296]{1,0:T(8,128)(2,1)S(1)}, bf16[16,7296]{1,0:T(8,128)(2,1)S(1)}, u32[]{:S(2)}, u32[]{:S(2)}) collective-permute-start(bf16[16,7296]{1,0:T(8,128)(2,1)S(1)} %pad_maximum_fusion.4), channel_id=1, source_target_pairs={{0,96},{1,33},{2,98},{3,35},{4,100},{5,37},{6,102},{7,39},{8,104},... | collective-permute-start | bytes 700424 | tf_op jit(solution)/shard_map/ppermute | solution.py:51
  85.2 3.4 %collective-permute-done.14 = bf16[16,7296]{1,0:T(8,128)(2,1)S(1)} collective-permute-done((bf16[16,7296]{1,0:T(8,128)(2,1)S(1)}, bf16[16,7296]{1,0:T(8,128)(2,1)S(1)}, u32[]{:S(2)}, u32[]{:S(2)}) %collective-permute-start.14) | collective-permute-done | bytes 233504 | tf_op jit(solution)/shard_map/ppermute | solution.py:51
  90.7 4.0 %collective-permute-done.15 = bf16[16,7296]{1,0:T(8,128)(2,1)S(1)} collective-permute-done((bf16[16,7296]{1,0:T(8,128)(2,1)S(1)}, bf16[16,7296]{1,0:T(8,128)(2,1)S(1)}, u32[]{:S(2)}, u32[]{:S(2)}) %collective-permute-start.15) | collective-permute-done | bytes 233504 | tf_op jit(solution)/shard_map/ppermute | solution.py:51
  97.1 11.3 %collective-permute-done.16 = bf16[32,7296]{1,0:T(8,128)(2,1)S(1)} collective-permute-done((bf16[32,7296]{1,0:T(8,128)(2,1)S(1)}, bf16[32,7296]{1,0:T(8,128)(2,1)S(1)}, u32[]{:S(2)}, u32[]{:S(2)}) %collective-permute-start.16) | collective-permute-done | bytes 466976 | tf_op jit(solution)/shard_map/ppermute | solution.py:51
  108.5 3.5 %collective-permute-done.13.refs_1_.refs_3_ = bf16[64,7296]{1,0:T(8,128)(2,1)} collective-permute-done((bf16[64,7296]{1,0:T(8,128)(2,1)S(1)}, bf16[64,7296]{1,0:T(8,128)(2,1)}, u32[]{:S(2)}, u32[]{:S(2)}) %collective-permute-start.13) | collective-permute-done | bytes 933920 | tf_op jit(solution)/shard_map/ppermute | solution.py:55
  112.0 2.6 collective-permute-start.22
  114.6 7.6 %collective-permute-done.17.refs_2_.refs_4_ = bf16[64,7296]{1,0:T(8,128)(2,1)} collective-permute-done((bf16[64,7296]{1,0:T(8,128)(2,1)S(1)}, bf16[64,7296]{1,0:T(8,128)(2,1)}, u32[]{:S(2)}, u32[]{:S(2)}) %collective-permute-start.17) | collective-permute-done | bytes 933920 | tf_op jit(solution)/shard_map/ppermute | solution.py:55
  122.9 14.0 %experts.4 = (bf16[64,7168]{1,0:T(8,128)(2,1)}, bf16[64,7168]{1,0:T(8,128)(2,1)}) custom-call(s32[2]{0:T(128)} %pad_add_fusion.refs_0_, bf16[64,7296]{1,0:T(8,128)(2,1)} %collective-permute-done.13.refs_1_.refs_3_, bf16[64,7296]{1,0:T(8,128)(2,1)} %collective-permute-done.17.refs_2_.refs_4_, bf16[64,7296]{1,0:T(8,128)(2,1)} %collective-permute-done.13.refs_1_.refs_3_, ...), custom_call_target="tpu_custom_call" | custom-call | tf_op jit(solution)/shard_map/experts/pallas_call | solution.py:200
  137.9 14.0 %experts.7 = (bf16[64,7168]{1,0:T(8,128)(2,1)}, bf16[64,7168]{1,0:T(8,128)(2,1)}) custom-call(s32[2]{0:T(128)} %pad_add_fusion.refs_0_, bf16[64,7296]{1,0:T(8,128)(2,1)} %copy-done, bf16[64,7296]{1,0:T(8,128)(2,1)} %copy-done.1, bf16[64,7296]{1,0:T(8,128)(2,1)} %copy-done, bf16[64,7296]{1,0:T(8,128)(2,1)} %copy-done.1, bf16[1,7168,256]{2,1,0:T(8,128)(2,1)} %refs_5_.7, ...), custom_call_target="tpu_custom_call" | custom-call | tf_op jit(solution)/shard_map/experts/pallas_call | solution.py:200
  152.0 4.0 %collective-permute-start.25 = (bf16[64,7296]{1,0:T(8,128)(2,1)S(1)}, bf16[64,7296]{1,0:T(8,128)(2,1)S(1)}, u32[]{:S(2)}, u32[]{:S(2)}) collective-permute-start(bf16[64,7296]{1,0:T(8,128)(2,1)S(1)} %collective-permute-done.22.refs_1_.refs_3_), channel_id=1, source_target_pairs={{0,8},{1,25},{2,10},{3,27},{4,12},{5,29},{6,14},{7,31},{8,16},{9,1... | collective-permute-start | bytes 2801672 | tf_op jit(solution)/shard_map/ppermute | solution.py:55
  156.0 14.0 %experts.5 = (bf16[64,7168]{1,0:T(8,128)(2,1)}, bf16[64,7168]{1,0:T(8,128)(2,1)}) custom-call(s32[2]{0:T(128)} %pad_add_fusion.refs_0_, bf16[64,7296]{1,0:T(8,128)(2,1)} %copy-done.2, bf16[64,7296]{1,0:T(8,128)(2,1)} %collective-permute-done.23.refs_2_.refs_4_, bf16[64,7296]{1,0:T(8,128)(2,1)} %copy-done.2, ...), custom_call_target="tpu_custom_call" | custom-call | tf_op jit(solution)/shard_map/experts/pallas_call | solution.py:200
  170.0 2.4 add_convert_fusion.2
  172.4 3.4 %collective-permute-start.31 = (bf16[64,7168]{1,0:T(8,128)(2,1)}, bf16[64,7168]{1,0:T(8,128)(2,1)}, u32[]{:S(2)}, u32[]{:S(2)}) collective-permute-start(bf16[64,7168]{1,0:T(8,128)(2,1)} %add_convert_fusion.2), channel_id=1, source_target_pairs={{0,2},{1,7},{2,4},{3,1},{4,6},{5,3},{6,0},{7,5},{8,10},{9,15},{10,... | collective-permute-start | bytes 2752520 | tf_op jit(solution)/shard_map/ppermute | solution.py:55
  179.8 17.2 %collective-permute-done.26.refs_2_.refs_4_ = bf16[64,7296]{1,0:T(8,128)(2,1)S(1)} collective-permute-done((bf16[64,7296]{1,0:T(8,128)(2,1)}, bf16[64,7296]{1,0:T(8,128)(2,1)S(1)}, u32[]{:S(2)}, u32[]{:S(2)}) %collective-permute-start.26) | collective-permute-done | bytes 933920 | tf_op jit(solution)/shard_map/ppermute | solution.py:55
  198.0 14.0 %experts.6 = (bf16[64,7168]{1,0:T(8,128)(2,1)}, bf16[64,7168]{1,0:T(8,128)(2,1)}) custom-call(s32[2]{0:T(128)} %pad_add_fusion.refs_0_, bf16[64,7296]{1,0:T(8,128)(2,1)} %copy-done.3, bf16[64,7296]{1,0:T(8,128)(2,1)} %copy-done.4, bf16[64,7296]{1,0:T(8,128)(2,1)} %copy-done.3, bf16[64,7296]{1,0:T(8,128)(2,1)} %copy-done.4, bf16[1,7168,256]{2,1,0:T(8,128)(2,1)} %refs_5_.7, ...), custom_call_target="tpu_custom_call" | custom-call | tf_op jit(solution)/shard_map/experts/pallas_call | solution.py:200
  213.7 2.4 collective-permute-start.32
  218.6 13.4 %collective-permute-done.32 = bf16[64,7168]{1,0:T(8,128)(2,1)S(1)} collective-permute-done((bf16[64,7168]{1,0:T(8,128)(2,1)S(1)}, bf16[64,7168]{1,0:T(8,128)(2,1)S(1)}, u32[]{:S(2)}, u32[]{:S(2)}) %collective-permute-start.32) | collective-permute-done | bytes 917536 | tf_op jit(solution)/shard_map/ppermute | solution.py:55
  234.4 6.5 %collective-permute-done.33 = bf16[32,7168]{1,0:T(8,128)(2,1)S(1)} collective-permute-done((bf16[32,7168]{1,0:T(8,128)(2,1)S(1)}, bf16[32,7168]{1,0:T(8,128)(2,1)S(1)}, u32[]{:S(2)}, u32[]{:S(2)}) %collective-permute-start.33) | collective-permute-done | bytes 458784 | tf_op jit(solution)/shard_map/ppermute | solution.py:51
  244.7 2.5 collective-permute-done.34
  247.2 5.0 %collective-permute-start.35 = (bf16[16,7168]{1,0:T(8,128)(2,1)S(1)}, bf16[16,7168]{1,0:T(8,128)(2,1)S(1)}, u32[]{:S(2)}, u32[]{:S(2)}) collective-permute-start(bf16[16,7168]{1,0:T(8,128)(2,1)S(1)} %add_convert_fusion.11), channel_id=1, source_target_pairs={{0,96},{1,33},{2,98},{3,35},{4,100},{5,37},{6,102},{7,39},{8,104},... | collective-permute-start | bytes 688136 | tf_op jit(solution)/shard_map/ppermute | solution.py:51
  252.2 4.0 %collective-permute-done.35 = bf16[16,7168]{1,0:T(8,128)(2,1)S(1)} collective-permute-done((bf16[16,7168]{1,0:T(8,128)(2,1)S(1)}, bf16[16,7168]{1,0:T(8,128)(2,1)S(1)}, u32[]{:S(2)}, u32[]{:S(2)}) %collective-permute-start.35) | collective-permute-done | bytes 229408 | tf_op jit(solution)/shard_map/ppermute | solution.py:51
  256.4 4.8 %collective-permute-done.36 = bf16[8,7168]{1,0:T(8,128)(2,1)S(1)} collective-permute-done((bf16[8,7168]{1,0:T(8,128)(2,1)S(1)}, bf16[8,7168]{1,0:T(8,128)(2,1)S(1)}, u32[]{:S(2)}, u32[]{:S(2)}) %collective-permute-start.36) | collective-permute-done | bytes 114720 | tf_op jit(solution)/shard_map/ppermute | solution.py:51
  (135 shorter events, 45.5 us)
Async XLA Ops:
  0.0 33.6 %collective-permute-start.1 = (bf16[4,128,7168]{2,1,0:T(8,128)(2,1)}, bf16[4,128,7168]{2,1,0:T(8,128)(2,1)}, u32[]{:S(2)}, u32[]{:S(2)}) collective-permute-start(bf16[4,128,7168]{2,1,0:T(8,128)(2,1)} %param.16), channel_id=1, source_target_pairs={{0,1},{1,0},{2,3},{3,2},{4,5},{5,4},{6,7},{7,6},{8,9},{9,8},{10,11... | collective-permute-start | bytes 22020104 | tf_op jit(solution)/shard_map/ppermute | solution.py:59
  8.0 22.4 %all-to-all-start = ((bf16[16,8,8,512]{3,2,1,0:T(8,128)(2,1)}), bf16[16,8,8,512]{3,2,1,0:T(8,128)(2,1)S(1)}, u32[]{:S(2)}, u32[]{:S(2)}) async-start(bf16[16,8,8,512]{3,2,1,0:T(8,128)(2,1)} %attend.1), calls=%async_computation | async-start | bytes 2097152 | tf_op jit(solution)/shard_map/all_to_all | solution.py:286
  15.7 15.5 %collective-permute-start = (bf16[4,512,128]{1,2,0:T(8,128)(2,1)S(1)}, bf16[4,512,128]{1,2,0:T(8,128)(2,1)S(1)}, u32[]{:S(2)}, u32[]{:S(2)}) collective-permute-start(bf16[4,512,128]{1,2,0:T(8,128)(2,1)S(1)} %copy.15), channel_id=1, source_target_pairs={{0,1},{1,0},{2,3},{3,2},{4,5},{5,4},{6,7},{7,6},{8,9},{9,8},{10,11... | collective-permute-start | bytes 1572872 | tf_op jit(solution)/shard_map/ppermute | solution.py:59
  42.8 8.6 %collective-permute-start.2 = (bf16[64,3584]{1,0:T(8,128)(2,1)S(1)}, bf16[64,3584]{1,0:T(8,128)(2,1)S(1)}, u32[]{:S(2)}, u32[]{:S(2)}) collective-permute-start(bf16[64,3584]{1,0:T(8,128)(2,1)S(1)} %slice.79), channel_id=1, source_target_pairs={{0,24},{1,9},{2,26},{3,11},{4,28},{5,13},{6,30},{7,15},{8,16},{9,1... | collective-permute-start | bytes 1376264 | tf_op jit(solution)/shard_map/ppermute | solution.py:51
  45.0 9.9 %collective-permute-start.6 = (bf16[64,3584]{1,0:T(8,128)(2,1)S(1)}, bf16[64,3584]{1,0:T(8,128)(2,1)S(1)}, u32[]{:S(2)}, u32[]{:S(2)}) collective-permute-start(bf16[64,3584]{1,0:T(8,128)(2,1)S(1)} %slice.87), channel_id=1, source_target_pairs={{0,6},{1,3},{2,4},{3,1},{4,2},{5,7},{6,0},{7,5},{8,14},{9,11},{10,... | collective-permute-start | bytes 1376264 | tf_op jit(solution)/shard_map/ppermute | solution.py:51
  51.5 7.4 %collective-permute-start.3 = (bf16[32,3584]{1,0:T(8,128)(2,1)S(1)}, bf16[32,3584]{1,0:T(8,128)(2,1)S(1)}, u32[]{:S(2)}, u32[]{:S(2)}) collective-permute-start(bf16[32,3584]{1,0:T(8,128)(2,1)S(1)} %slice.105), channel_id=1, source_target_pairs={{0,8},{1,25},{2,10},{3,27},{4,12},{5,29},{6,14},{7,31},{8,0},{9,17... | collective-permute-start | bytes 688136 | tf_op jit(solution)/shard_map/ppermute | solution.py:51
  55.1 6.9 %collective-permute-start.7 = (bf16[32,3584]{1,0:T(8,128)(2,1)S(1)}, bf16[32,3584]{1,0:T(8,128)(2,1)S(1)}, u32[]{:S(2)}, u32[]{:S(2)}) collective-permute-start(bf16[32,3584]{1,0:T(8,128)(2,1)S(1)} %slice.111), channel_id=1, source_target_pairs={{0,2},{1,7},{2,0},{3,5},{4,6},{5,3},{6,4},{7,1},{8,10},{9,15},{10,... | collective-permute-start | bytes 688136 | tf_op jit(solution)/shard_map/ppermute | solution.py:51
  64.1 6.5 %collective-permute-start.5 = (bf16[8,3584]{1,0:T(8,128)(2,1)S(1)}, bf16[8,3584]{1,0:T(8,128)(2,1)S(1)}, u32[]{:S(2)}, u32[]{:S(2)}) collective-permute-start(bf16[8,3584]{1,0:T(8,128)(2,1)S(1)} %slice.109), channel_id=1, source_target_pairs={{0,2},{1,7},{2,0},{3,5},{4,6},{5,3},{6,4},{7,1},{8,10},{9,15},{10,... | collective-permute-start | bytes 172040 | tf_op jit(solution)/shard_map/ppermute | solution.py:51
  78.0 6.6 %collective-permute-start.11 = (bf16[16,7296]{1,0:T(8,128)(2,1)S(1)}, bf16[16,7296]{1,0:T(8,128)(2,1)S(1)}, u32[]{:S(2)}, u32[]{:S(2)}) collective-permute-start(bf16[16,7296]{1,0:T(8,128)(2,1)S(1)} %pad_maximum_fusion.4), channel_id=1, source_target_pairs={{0,2},{1,7},{2,0},{3,5},{4,6},{5,3},{6,4},{7,1},{8,10},{9,15},{10,... | collective-permute-start | bytes 700424 | tf_op jit(solution)/shard_map/ppermute | solution.py:51
  80.1 42.8 %collective-permute-start.18 = (bf16[1,7168,256]{2,1,0:T(8,128)(2,1)}, bf16[1,7168,256]{2,1,0:T(8,128)(2,1)}, u32[]{:S(2)}, u32[]{:S(2)}) collective-permute-start(bf16[1,7168,256]{2,1,0:T(8,128)(2,1)} %refs_5_.7), channel_id=1, source_target_pairs={{0,1},{1,0},{2,3},{3,2},{4,5},{5,4},{6,7},{7,6},{8,9},{9,8},{10,11... | collective-permute-start | bytes 11010056 | tf_op jit(solution)/shard_map/ppermute | solution.py:59
  80.1 42.8 %collective-permute-start.19 = (bf16[1,7168,256]{2,1,0:T(8,128)(2,1)}, bf16[1,7168,256]{2,1,0:T(8,128)(2,1)}, u32[]{:S(2)}, u32[]{:S(2)}) collective-permute-start(bf16[1,7168,256]{2,1,0:T(8,128)(2,1)} %refs_7_.7), channel_id=1, source_target_pairs={{0,1},{1,0},{2,3},{3,2},{4,5},{5,4},{6,7},{7,6},{8,9},{9,8},{10,11... | collective-permute-start | bytes 11010056 | tf_op jit(solution)/shard_map/ppermute | solution.py:59
  80.6 42.3 %collective-permute-start.20 = (bf16[1,256,7168]{2,1,0:T(8,128)(2,1)}, bf16[1,256,7168]{2,1,0:T(8,128)(2,1)}, u32[]{:S(2)}, u32[]{:S(2)}) collective-permute-start(bf16[1,256,7168]{2,1,0:T(8,128)(2,1)} %refs_9_.7), channel_id=1, source_target_pairs={{0,1},{1,0},{2,3},{3,2},{4,5},{5,4},{6,7},{7,6},{8,9},{9,8},{10,11... | collective-permute-start | bytes 11010056 | tf_op jit(solution)/shard_map/ppermute | solution.py:59
  80.6 8.1 %collective-permute-start.14 = (bf16[16,7296]{1,0:T(8,128)(2,1)S(1)}, bf16[16,7296]{1,0:T(8,128)(2,1)S(1)}, u32[]{:S(2)}, u32[]{:S(2)}) collective-permute-start(bf16[16,7296]{1,0:T(8,128)(2,1)S(1)} %pad_maximum_fusion.4), channel_id=1, source_target_pairs={{0,96},{1,33},{2,98},{3,35},{4,100},{5,37},{6,102},{7,39},{8,104},... | collective-permute-start | bytes 700424 | tf_op jit(solution)/shard_map/ppermute | solution.py:51
  84.6 11.3 %collective-permute-start.12 = (bf16[32,7296]{1,0:T(8,128)(2,1)S(1)}, bf16[32,7296]{1,0:T(8,128)(2,1)S(1)}, u32[]{:S(2)}, u32[]{:S(2)}) collective-permute-start(bf16[32,7296]{1,0:T(8,128)(2,1)S(1)} %pad_maximum_fusion.1), channel_id=1, source_target_pairs={{0,6},{1,3},{2,4},{3,1},{4,2},{5,7},{6,0},{7,5},{8,14},{9,11},{10,... | collective-permute-start | bytes 1400840 | tf_op jit(solution)/shard_map/ppermute | solution.py:51
  94.8 13.6 %collective-permute-start.16 = (bf16[32,7296]{1,0:T(8,128)(2,1)S(1)}, bf16[32,7296]{1,0:T(8,128)(2,1)S(1)}, u32[]{:S(2)}, u32[]{:S(2)}) collective-permute-start(bf16[32,7296]{1,0:T(8,128)(2,1)S(1)} %pad_maximum_fusion.2), channel_id=1, source_target_pairs={{0,24},{1,9},{2,26},{3,11},{4,28},{5,13},{6,30},{7,15},{8,16},{9,1... | collective-permute-start | bytes 1400840 | tf_op jit(solution)/shard_map/ppermute | solution.py:51
  96.1 16.0 %collective-permute-start.13 = (bf16[64,7296]{1,0:T(8,128)(2,1)S(1)}, bf16[64,7296]{1,0:T(8,128)(2,1)}, u32[]{:S(2)}, u32[]{:S(2)}) collective-permute-start(bf16[64,7296]{1,0:T(8,128)(2,1)S(1)} %pad_maximum_fusion.refs_1_.refs_3_), channel_id=1, source_target_pairs={{0,8},{1,25},{2,10},{3,27},{4,12},{5,29},{6,14},{7,31},{8,16},{9,1... | collective-permute-start | bytes 2801672 | tf_op jit(solution)/shard_map/ppermute | solution.py:55
  108.5 13.7 %collective-permute-start.17 = (bf16[64,7296]{1,0:T(8,128)(2,1)S(1)}, bf16[64,7296]{1,0:T(8,128)(2,1)}, u32[]{:S(2)}, u32[]{:S(2)}) collective-permute-start(bf16[64,7296]{1,0:T(8,128)(2,1)S(1)} %constant_dynamic-update-slice_fusion.refs_2_.refs_4_), channel_id=1, source_target_pairs={{0,2},{1,7},{2,4},{3,1},{4,6},{5,3},{6,0},{7,5},{8,10},{9,15},{10,... | collective-permute-start | bytes 2801672 | tf_op jit(solution)/shard_map/ppermute | solution.py:55
  112.0 40.0 %collective-permute-start.22 = (bf16[64,7296]{1,0:T(8,128)(2,1)}, bf16[64,7296]{1,0:T(8,128)(2,1)S(1)}, u32[]{:S(2)}, u32[]{:S(2)}) collective-permute-start(bf16[64,7296]{1,0:T(8,128)(2,1)} %collective-permute-done.13.refs_1_.refs_3_), channel_id=1, source_target_pairs={{0,8},{1,25},{2,10},{3,27},{4,12},{5,29},{6,14},{7,31},{8,16},{9,1... | collective-permute-start | bytes 2801672 | tf_op jit(solution)/shard_map/ppermute | solution.py:55
  122.2 33.8 %collective-permute-start.23 = (bf16[64,7296]{1,0:T(8,128)(2,1)}, bf16[64,7296]{1,0:T(8,128)(2,1)}, u32[]{:S(2)}, u32[]{:S(2)}) collective-permute-start(bf16[64,7296]{1,0:T(8,128)(2,1)} %collective-permute-done.17.refs_2_.refs_4_), channel_id=1, source_target_pairs={{0,2},{1,7},{2,4},{3,1},{4,6},{5,3},{6,0},{7,5},{8,10},{9,15},{10,... | collective-permute-start | bytes 2801672 | tf_op jit(solution)/shard_map/ppermute | solution.py:55
  136.9 33.1 %collective-permute-start.30 = (bf16[64,7168]{1,0:T(8,128)(2,1)}, bf16[64,7168]{1,0:T(8,128)(2,1)S(1)}, u32[]{:S(2)}, u32[]{:S(2)}) collective-permute-start(bf16[64,7168]{1,0:T(8,128)(2,1)} %get-tuple-element.21), channel_id=1, source_target_pairs={{0,2},{1,7},{2,4},{3,1},{4,6},{5,3},{6,0},{7,5},{8,10},{9,15},{10,... | collective-permute-start | bytes 2752520 | tf_op jit(solution)/shard_map/ppermute | solution.py:55
  151.9 24.5 %collective-permute-start.21 = (bf16[64,7168]{1,0:T(8,128)(2,1)}, bf16[64,7168]{1,0:T(8,128)(2,1)}, u32[]{:S(2)}, u32[]{:S(2)}) collective-permute-start(bf16[64,7168]{1,0:T(8,128)(2,1)} %get-tuple-element.17), channel_id=1, source_target_pairs={{0,8},{1,25},{2,10},{3,27},{4,12},{5,29},{6,14},{7,31},{8,16},{9,1... | collective-permute-start | bytes 2752520 | tf_op jit(solution)/shard_map/ppermute | solution.py:55
  152.0 27.7 %collective-permute-start.25 = (bf16[64,7296]{1,0:T(8,128)(2,1)S(1)}, bf16[64,7296]{1,0:T(8,128)(2,1)S(1)}, u32[]{:S(2)}, u32[]{:S(2)}) collective-permute-start(bf16[64,7296]{1,0:T(8,128)(2,1)S(1)} %collective-permute-done.22.refs_1_.refs_3_), channel_id=1, source_target_pairs={{0,8},{1,25},{2,10},{3,27},{4,12},{5,29},{6,14},{7,31},{8,16},{9,1... | collective-permute-start | bytes 2801672 | tf_op jit(solution)/shard_map/ppermute | solution.py:55
  172.4 39.5 %collective-permute-start.31 = (bf16[64,7168]{1,0:T(8,128)(2,1)}, bf16[64,7168]{1,0:T(8,128)(2,1)}, u32[]{:S(2)}, u32[]{:S(2)}) collective-permute-start(bf16[64,7168]{1,0:T(8,128)(2,1)} %add_convert_fusion.2), channel_id=1, source_target_pairs={{0,2},{1,7},{2,4},{3,1},{4,6},{5,3},{6,0},{7,5},{8,10},{9,15},{10,... | collective-permute-start | bytes 2752520 | tf_op jit(solution)/shard_map/ppermute | solution.py:55
  175.8 21.2 %collective-permute-start.26 = (bf16[64,7296]{1,0:T(8,128)(2,1)}, bf16[64,7296]{1,0:T(8,128)(2,1)S(1)}, u32[]{:S(2)}, u32[]{:S(2)}) collective-permute-start(bf16[64,7296]{1,0:T(8,128)(2,1)} %collective-permute-done.23.refs_2_.refs_4_), channel_id=1, source_target_pairs={{0,2},{1,7},{2,4},{3,1},{4,6},{5,3},{6,0},{7,5},{8,10},{9,15},{10,... | collective-permute-start | bytes 2801672 | tf_op jit(solution)/shard_map/ppermute | solution.py:55
  178.7 37.4 %collective-permute-start.24 = (bf16[64,7168]{1,0:T(8,128)(2,1)}, bf16[64,7168]{1,0:T(8,128)(2,1)}, u32[]{:S(2)}, u32[]{:S(2)}) collective-permute-start(bf16[64,7168]{1,0:T(8,128)(2,1)} %add_convert_fusion.5), channel_id=1, source_target_pairs={{0,8},{1,25},{2,10},{3,27},{4,12},{5,29},{6,14},{7,31},{8,16},{9,1... | collective-permute-start | bytes 2752520 | tf_op jit(solution)/shard_map/ppermute | solution.py:55
  213.7 18.4 %collective-permute-start.32 = (bf16[64,7168]{1,0:T(8,128)(2,1)S(1)}, bf16[64,7168]{1,0:T(8,128)(2,1)S(1)}, u32[]{:S(2)}, u32[]{:S(2)}) collective-permute-start(bf16[64,7168]{1,0:T(8,128)(2,1)S(1)} %add_convert_fusion.1), channel_id=1, source_target_pairs={{0,2},{1,7},{2,4},{3,1},{4,6},{5,3},{6,0},{7,5},{8,10},{9,15},{10,... | collective-permute-start | bytes 2752520 | tf_op jit(solution)/shard_map/ppermute | solution.py:55
  217.6 15.9 %collective-permute-start.27 = (bf16[64,7168]{1,0:T(8,128)(2,1)S(1)}, bf16[64,7168]{1,0:T(8,128)(2,1)S(1)}, u32[]{:S(2)}, u32[]{:S(2)}) collective-permute-start(bf16[64,7168]{1,0:T(8,128)(2,1)S(1)} %add_convert_fusion.4), channel_id=1, source_target_pairs={{0,8},{1,25},{2,10},{3,27},{4,12},{5,29},{6,14},{7,31},{8,16},{9,1... | collective-permute-start | bytes 2752520 | tf_op jit(solution)/shard_map/ppermute | solution.py:55
  232.4 8.6 %collective-permute-start.33 = (bf16[32,7168]{1,0:T(8,128)(2,1)S(1)}, bf16[32,7168]{1,0:T(8,128)(2,1)S(1)}, u32[]{:S(2)}, u32[]{:S(2)}) collective-permute-start(bf16[32,7168]{1,0:T(8,128)(2,1)S(1)} %slice.121), channel_id=1, source_target_pairs={{0,24},{1,9},{2,26},{3,11},{4,28},{5,13},{6,30},{7,15},{8,16},{9,1... | collective-permute-start | bytes 1376264 | tf_op jit(solution)/shard_map/ppermute | solution.py:51
  233.7 8.6 %collective-permute-start.28 = (bf16[32,7168]{1,0:T(8,128)(2,1)S(1)}, bf16[32,7168]{1,0:T(8,128)(2,1)S(1)}, u32[]{:S(2)}, u32[]{:S(2)}) collective-permute-start(bf16[32,7168]{1,0:T(8,128)(2,1)S(1)} %slice.117), channel_id=1, source_target_pairs={{0,6},{1,3},{2,4},{3,1},{4,2},{5,7},{6,0},{7,5},{8,14},{9,11},{10,... | collective-permute-start | bytes 1376264 | tf_op jit(solution)/shard_map/ppermute | solution.py:51
  241.0 6.1 %collective-permute-start.34 = (bf16[16,7168]{1,0:T(8,128)(2,1)S(1)}, bf16[16,7168]{1,0:T(8,128)(2,1)S(1)}, u32[]{:S(2)}, u32[]{:S(2)}) collective-permute-start(bf16[16,7168]{1,0:T(8,128)(2,1)S(1)} %slice.123), channel_id=1, source_target_pairs={{0,8},{1,25},{2,10},{3,27},{4,12},{5,29},{6,14},{7,31},{8,0},{9,17... | collective-permute-start | bytes 688136 | tf_op jit(solution)/shard_map/ppermute | solution.py:51
  242.4 9.8 %collective-permute-start.29 = (bf16[16,7168]{1,0:T(8,128)(2,1)S(1)}, bf16[16,7168]{1,0:T(8,128)(2,1)S(1)}, u32[]{:S(2)}, u32[]{:S(2)}) collective-permute-start(bf16[16,7168]{1,0:T(8,128)(2,1)S(1)} %slice.119), channel_id=1, source_target_pairs={{0,2},{1,7},{2,0},{3,5},{4,6},{5,3},{6,4},{7,1},{8,10},{9,15},{10,... | collective-permute-start | bytes 688136 | tf_op jit(solution)/shard_map/ppermute | solution.py:51
  247.2 9.0 %collective-permute-start.35 = (bf16[16,7168]{1,0:T(8,128)(2,1)S(1)}, bf16[16,7168]{1,0:T(8,128)(2,1)S(1)}, u32[]{:S(2)}, u32[]{:S(2)}) collective-permute-start(bf16[16,7168]{1,0:T(8,128)(2,1)S(1)} %add_convert_fusion.11), channel_id=1, source_target_pairs={{0,96},{1,33},{2,98},{3,35},{4,100},{5,37},{6,102},{7,39},{8,104},... | collective-permute-start | bytes 688136 | tf_op jit(solution)/shard_map/ppermute | solution.py:51
  (21 other events, 222.2 us)
